TPU v7x, 32 devices: a whole 2x2x4 slice. The times are simulated.
32 devices in a mesh: dp: 16 (over z, y, x), tensor: 2 (over core).
Axes of the slice: x: 2, y: 2, z: 4, core: 2. Of those that a mesh axis runs over, the one named last changes fastest.
Arguments:
- tokens: bfloat16 [16, 2048, 512], P('dp', 'tensor'), may hold values from -6 to 6
- cotangent: bfloat16 [16, 2048, 512], P('dp', 'tensor'), may hold values from -6 to 6
- span_ids: int32 [16, 8, 256], P('dp'), may hold values from 0 to 1, never falling along the last dimension, each value on 1 to 192 neighbouring positions
- gain_one: float32 [512], replicated, may hold values from 0.25 to 1.75
- w_qkv: bfloat16 [512, 3, 512], P('dp', None, 'tensor'), may hold values from -0.25 to 0.25
- w_out: bfloat16 [512, 512], P('tensor', 'dp'), may hold values from -1 to 1
- b_out: float32 [512], replicated, may hold values from -3 to 3
- gain_two: float32 [512], replicated, may hold values from 0.25 to 1.75
- w_up: bfloat16 [512, 2048], P('dp', 'tensor'), may hold values from -0.25 to 0.25
- b_up: float32 [2048], P('tensor'), may hold values from -3 to 3
- w_down: bfloat16 [2048, 512], P('tensor', 'dp'), may hold values from -0.125 to 0.125
- b_down: float32 [512], replicated, may hold values from -3 to 3
Outputs:
- result: bfloat16 [16, 2048, 512], P('dp', 'tensor')
- d_tokens: bfloat16 [16, 2048, 512], P('dp', 'tensor')
- d_gain_one: float32 [512], replicated
- d_w_qkv: float32 [512, 3, 512], P('dp', None, 'tensor')
- d_w_out: float32 [512, 512], P('tensor', 'dp')
- d_b_out: float32 [512], replicated
- d_gain_two: float32 [512], replicated
- d_w_up: float32 [512, 2048], P('dp', 'tensor')
- d_b_up: float32 [2048], replicated
- d_w_down: float32 [2048, 512], P('tensor', 'dp')
- d_b_down: float32 [512], replicated
Inputs may be any that keep to these rules, and one draw needn't show every extreme that they name: `span_ids`: within each block of 256 positions the span numbers never fall and each of the 2 spans holds 1 to 192 positions.
All inputs are finite; a program needn't handle non-finite values.
Results may differ from a plain program's by a relative error of at most 0.014.
Values may be sent and summed in bfloat16 or wider, within the bound.
A program may use at most 128 MiB of HBM per device.

v0:
```python
import math
import jax
import jax.numpy as jnp
from jax import lax
from jax.sharding import PartitionSpec as P

HD = 64
BLK = 256
SPB = 2
epsilon = 1e-05
masked = -1e30


def normalize(values, gain_vec):
    centre = values - jnp.mean(values, axis=-1, keepdims=True)
    spread = jnp.mean(centre * centre, axis=-1, keepdims=True)
    inverse = lax.rsqrt(spread + epsilon)
    unit_rows = centre * inverse
    return (unit_rows, inverse, unit_rows * gain_vec)


def normalize_back(incoming_grad, unit_rows, inverse, gain_vec):
    scaled = incoming_grad * gain_vec
    mean_one = jnp.mean(scaled, axis=-1, keepdims=True)
    mean_two = jnp.mean(scaled * unit_rows, axis=-1, keepdims=True)
    return (
        inverse * (scaled - mean_one - unit_rows * mean_two),
        jnp.sum(incoming_grad * unit_rows, axis=0),
    )


def pair_rows(values):
    return lax.all_gather(values, "tensor", axis=0, tiled=True)


def pair_sums(term_fn, rows):
    return lax.psum_scatter(
        term_fn(jnp.int32(0), rows * lax.axis_size("tensor")).astype(jnp.bfloat16),
        "tensor",
        scatter_dimension=0,
        tiled=True,
    ).astype(jnp.float32)


def scores(queries, key_rows, key_sum, counts_all, allowed):
    scaling = 1.0 / math.sqrt(queries.shape[-1])
    near_scores = (
        jnp.einsum("bie,bje->bij", queries, key_rows, preferred_element_type=jnp.float32) * scaling
    )
    far_scores = (
        jnp.einsum("bie,ce->bic", queries, key_sum, preferred_element_type=jnp.float32) * scaling
    )
    far_scores = far_scores + jnp.log(counts_all).reshape(-1)
    far_scores = jnp.where(allowed[:, None, :], far_scores, masked)
    return (near_scores, far_scores)


def span_means(key_rows, value_rows, member_low, counts):
    head_size = key_rows.shape[-1]
    key_sum = jnp.einsum("bjm,bje->bme", member_low, key_rows, preferred_element_type=jnp.float32)
    value_sum = jnp.einsum(
        "bjm,bje->bme", member_low, value_rows, preferred_element_type=jnp.float32
    )
    key_sum = (key_sum / counts[:, :, None]).astype(jnp.bfloat16).reshape(-1, head_size)
    value_sum = (value_sum / counts[:, :, None]).astype(jnp.bfloat16).reshape(-1, head_size)
    return (key_sum, value_sum)


def attend(queries, key_rows, value_rows, key_sum, value_sum, counts_all, allowed):
    near_scores, far_scores = scores(queries, key_rows, key_sum, counts_all, allowed)
    largest = jnp.maximum(jnp.max(near_scores, axis=-1), jnp.max(far_scores, axis=-1))
    near_exp = jnp.exp(near_scores - largest[..., None])
    far_exp = jnp.exp(far_scores - largest[..., None])
    denominator = jnp.sum(near_exp, axis=-1) + jnp.sum(far_exp, axis=-1)
    near_prob = (near_exp / denominator[..., None]).astype(jnp.bfloat16)
    far_prob = (far_exp / denominator[..., None]).astype(jnp.bfloat16)
    attended = jnp.einsum("bij,bje->bie", near_prob, value_rows, preferred_element_type=jnp.float32)
    attended = attended + jnp.einsum(
        "bic,ce->bie", far_prob, value_sum, preferred_element_type=jnp.float32
    )
    return (attended.astype(jnp.bfloat16), largest + jnp.log(denominator))


def head_backward(
    queries, key_rows, value_rows, grad_heads, log_total, key_sum, value_sum, counts_all, allowed
):
    scaling = 1.0 / math.sqrt(queries.shape[-1])
    near_scores, far_scores = scores(queries, key_rows, key_sum, counts_all, allowed)
    near_prob = jnp.exp(near_scores - log_total[..., None])
    far_prob = jnp.exp(far_scores - log_total[..., None])
    grad_value = jnp.einsum(
        "bij,bie->bje",
        near_prob.astype(jnp.bfloat16),
        grad_heads,
        preferred_element_type=jnp.float32,
    )
    grad_vsum = jnp.einsum(
        "bic,bie->ce", far_prob.astype(jnp.bfloat16), grad_heads, preferred_element_type=jnp.float32
    )
    near_dprob = jnp.einsum(
        "bie,bje->bij", grad_heads, value_rows, preferred_element_type=jnp.float32
    )
    far_dprob = jnp.einsum("bie,ce->bic", grad_heads, value_sum, preferred_element_type=jnp.float32)
    correction = jnp.sum(near_prob * near_dprob, axis=-1) + jnp.sum(far_prob * far_dprob, axis=-1)
    near_grad = (near_prob * (near_dprob - correction[..., None])).astype(jnp.bfloat16)
    far_grad = (far_prob * (far_dprob - correction[..., None])).astype(jnp.bfloat16)
    grad_query = jnp.einsum("bij,bje->bie", near_grad, key_rows, preferred_element_type=jnp.float32)
    grad_query = (
        grad_query
        + jnp.einsum("bic,ce->bie", far_grad, key_sum, preferred_element_type=jnp.float32)
    ) * scaling
    grad_key = (
        jnp.einsum("bij,bie->bje", near_grad, queries, preferred_element_type=jnp.float32) * scaling
    )
    grad_ksum = (
        jnp.einsum("bic,bie->ce", far_grad, queries, preferred_element_type=jnp.float32) * scaling
    )
    return (grad_query.astype(jnp.bfloat16), grad_key, grad_value, grad_ksum, grad_vsum)


def shards(
    tokens, cotangent, span_ids, gain_one, w_qkv, w_out, b_out, gain_two, w_up, b_up, w_down, b_down
):
    incoming = tokens[0].astype(jnp.float32)
    row_count = incoming.shape[0]
    full_qkv, full_out, full_up, full_down = (
        lax.all_gather(w_qkv, "dp", axis=0, tiled=True),
        lax.all_gather(w_out, "dp", axis=1, tiled=True),
        lax.all_gather(w_up, "dp", axis=0, tiled=True),
        lax.all_gather(w_down, "dp", axis=1, tiled=True),
    )
    unit_one, inverse_one, normed = normalize(incoming, gain_one)
    normed_low = normed.astype(jnp.bfloat16)
    span_all = span_ids[0]
    member_all = (span_all[:, :, None] == jnp.arange(SPB, dtype=jnp.int32)[None, None, :]).astype(
        jnp.float32
    )
    counts_all = jnp.sum(member_all, axis=1)
    total_blocks = span_all.shape[0]
    qkv_whole, out_whole, up_whole, down_whole, bias_whole = (
        full_qkv,
        full_out,
        full_up,
        full_down,
        b_up,
    )
    rows_one = pair_rows(normed_low)
    width = qkv_whole.shape[0]
    qkv_flat = qkv_whole.reshape(width, -1)
    length = rows_one.shape[0]
    blocks = length // BLK
    heads_here = qkv_whole.shape[2] // HD
    projected = jnp.dot(rows_one, qkv_flat, preferred_element_type=jnp.float32).astype(jnp.bfloat16)
    per_head = jnp.moveaxis(projected.reshape(blocks, BLK, 3, heads_here, HD), (2, 3), (0, 1))
    member_low = member_all.astype(jnp.bfloat16)
    allowed = jnp.arange(blocks)[:, None] > (jnp.arange(total_blocks * SPB) // SPB)[None, :]
    key_sums, value_sums = lax.map(
        lambda pieces: span_means(pieces[0], pieces[1], member_low, counts_all),
        (per_head[1], per_head[2]),
    )

    def forward_head(pieces):
        return attend(pieces[0], pieces[1], pieces[2], pieces[3], pieces[4], counts_all, allowed)

    attended, log_total = lax.map(
        forward_head, (per_head[0], per_head[1], per_head[2], key_sums, value_sums)
    )
    attended_flat = jnp.moveaxis(attended, 0, 2).reshape(length, -1)

    def project_attn(offset, amount):
        return jnp.dot(attended_flat, out_whole, preferred_element_type=jnp.float32)

    attn_total = pair_sums(project_attn, row_count)
    middle = incoming + (attn_total + b_out)
    unit_two, inverse_two, normed_two = normalize(middle, gain_two)
    rows_two = pair_rows(normed_two.astype(jnp.bfloat16))
    before_gelu = jnp.dot(rows_two, up_whole, preferred_element_type=jnp.float32) + bias_whole
    activated, gelu_pull = jax.vjp(jax.nn.gelu, before_gelu)
    hidden = activated.astype(jnp.bfloat16)

    def project_mlp(offset, amount):
        return jnp.dot(hidden, down_whole, preferred_element_type=jnp.float32)

    mlp_total = pair_sums(project_mlp, row_count)
    output = middle + (mlp_total + b_down)
    grad_rows = cotangent[0]
    grad_output = grad_rows.astype(jnp.float32)
    full_grad = pair_rows(grad_rows)
    grad_down = jnp.einsum("sf,sd->fd", hidden, full_grad, preferred_element_type=jnp.float32)
    grad_hidden = jnp.einsum("sd,fd->sf", full_grad, down_whole, preferred_element_type=jnp.float32)
    grad_inner = gelu_pull(grad_hidden)[0].astype(jnp.bfloat16)
    bias_up = jnp.sum(grad_inner, axis=0, dtype=jnp.float32)
    grad_up = jnp.einsum("sd,sf->df", rows_two, grad_inner, preferred_element_type=jnp.float32)

    def back_mlp_rows(offset, amount):
        return jnp.einsum("sf,df->sd", grad_inner, up_whole, preferred_element_type=jnp.float32)

    grad_second = pair_sums(back_mlp_rows, row_count)
    grad_norm_two, gain_two_part = normalize_back(grad_second, unit_two, inverse_two, gain_two)
    grad_mid = grad_output + grad_norm_two
    grad_branch = grad_mid.astype(jnp.bfloat16)
    full_branch = pair_rows(grad_branch)
    grad_wout = jnp.einsum(
        "sh,sd->hd", attended_flat, full_branch, preferred_element_type=jnp.float32
    )
    grad_attended = jnp.einsum(
        "sd,hd->sh", full_branch, out_whole, preferred_element_type=jnp.float32
    ).astype(jnp.bfloat16)
    grad_heads = jnp.moveaxis(grad_attended.reshape(blocks, BLK, heads_here, HD), 2, 0)

    def backward_head(pieces):
        return head_backward(
            pieces[0],
            pieces[1],
            pieces[2],
            pieces[3],
            pieces[4],
            pieces[5],
            pieces[6],
            counts_all,
            allowed,
        )

    grad_query, grad_key, grad_value, grad_ksums, grad_vsums = lax.map(
        backward_head,
        (per_head[0], per_head[1], per_head[2], grad_heads, log_total, key_sums, value_sums),
    )
    share_key = grad_ksums.reshape(heads_here, blocks, SPB, HD) / counts_all[None, :, :, None]
    share_value = grad_vsums.reshape(heads_here, blocks, SPB, HD) / counts_all[None, :, :, None]
    grad_key = (grad_key + jnp.einsum("bjm,hbme->hbje", member_all, share_key)).astype(jnp.bfloat16)
    grad_value = (grad_value + jnp.einsum("bjm,hbme->hbje", member_all, share_value)).astype(
        jnp.bfloat16
    )
    grad_projected = jnp.moveaxis(
        jnp.stack((grad_query, grad_key, grad_value), axis=0), (0, 1), (2, 3)
    ).reshape(length, -1)
    grad_qkv = jnp.einsum(
        "sd,sc->dc", rows_one, grad_projected, preferred_element_type=jnp.float32
    ).reshape(qkv_whole.shape)

    def back_attn_rows(offset, amount):
        return jnp.einsum("sc,dc->sd", grad_projected, qkv_flat, preferred_element_type=jnp.float32)

    grad_first = pair_sums(back_attn_rows, row_count)
    grad_norm_one, gain_one_part = normalize_back(grad_first, unit_one, inverse_one, gain_one)
    grad_input = grad_mid + grad_norm_one
    half_width = bias_up.shape[0]
    bias_up_full = lax.dynamic_update_slice(
        jnp.zeros((half_width * lax.axis_size("tensor"),), jnp.float32),
        bias_up,
        (lax.axis_index("tensor") * half_width,),
    )
    totals = lax.psum(
        (
            gain_one_part,
            gain_two_part,
            jnp.sum(grad_branch, axis=0, dtype=jnp.float32),
            jnp.sum(grad_output, axis=0),
            bias_up_full,
        ),
        ("dp", "tensor"),
    )
    grad_qkv, grad_wout, grad_up, grad_down = (
        lax.psum_scatter(grad_qkv, "dp", scatter_dimension=0, tiled=True),
        lax.psum_scatter(grad_wout, "dp", scatter_dimension=1, tiled=True),
        lax.psum_scatter(grad_up, "dp", scatter_dimension=0, tiled=True),
        lax.psum_scatter(grad_down, "dp", scatter_dimension=1, tiled=True),
    )
    factor = 1.0 / math.sqrt(lax.axis_size("dp") * lax.axis_size("tensor") * row_count)
    return (
        output.astype(jnp.bfloat16)[None],
        grad_input.astype(jnp.bfloat16)[None],
        totals[0] * factor,
        grad_qkv * factor,
        grad_wout * factor,
        totals[2] * factor,
        totals[1] * factor,
        grad_up * factor,
        totals[4] * factor,
        grad_down * factor,
        totals[3] * factor,
    )


def solution(mesh):
    in_specs = (
        P("dp", "tensor", None),
        P("dp", "tensor", None),
        P("dp", None, None),
        P(),
        P("dp", None, "tensor"),
        P("tensor", "dp"),
        P(),
        P(),
        P("dp", "tensor"),
        P("tensor"),
        P("tensor", "dp"),
        P(),
    )
    out_specs = (
        P("dp", "tensor", None),
        P("dp", "tensor", None),
        P(),
        P("dp", None, "tensor"),
        P("tensor", "dp"),
        P(),
        P(),
        P("dp", "tensor"),
        P(),
        P("tensor", "dp"),
        P(),
    )
    return jax.shard_map(shards, mesh=mesh, in_specs=in_specs, out_specs=out_specs, check_vma=False)
```

profile of v0, /device:TPU:0, one launch (start us, length us, event | category | flops | bytes accessed | tf_op | source)
XLA Modules:
  0.0 714.1 jit_solution(7615604891802510770)
XLA Ops:
  13.1 47.0 %all_gather.25 = bf16[512,3,256]{2,0,1:T(8,128)(2,1)S(1)} all-gather(bf16[32,3,256]{2,0,1:T(8,128)(2,1)S(1)} %copy-done.14), channel_id=1, replica_groups=mesh['dp'=16,'tensor'=2] {'dp'}, dimensions={0}, use_global_device_ids=true | all-gather | bytes 835584 | tf_op jit(solution)/shard_map/all_gather | solution.py:127
  60.4 36.9 %all_gather.26 = bf16[256,512]{0,1:T(8,128)(2,1)S(1)} all-gather(bf16[256,32]{0,1:T(8,128)(2,1)S(1)} %copy-done.18), channel_id=1, replica_groups=mesh['dp'=16,'tensor'=2] {'dp'}, dimensions={1}, use_global_device_ids=true | all-gather | bytes 278528 | tf_op jit(solution)/shard_map/all_gather | solution.py:128
  97.3 5.1 convolution_convert_fusion
  102.4 4.7 copy.64
  107.1 3.0 copy.111
  115.9 14.6 %while.50 = (s32[]{:T(128)}, bf16[4,8,256,64]{2,3,1,0:T(8,128)(2,1)}, f32[4,8,256]{2,1,0:T(8,128)S(1)}, bf16[4,8,256,64]{2,3,1,0:T(8,128)(2,1)S(1)}, bf16[4,8,25...) while((s32[]{:T(128)}, ...), condition=%wide.region_10.11_spmd.clone, body=%wide.region_5.10_spmd.clone.sunk | while | flops 147880064 | bytes 9204541 | solution.py:165
  136.7 6.9 reduce-scatter.9.cloned.1.call-done
  149.1 43.8 %all-gather.12.cloned.1.call-done = bf16[512,1024]{1,0:T(8,128)(2,1)} async-done(((bf16[32,1024]{1,0:T(8,128)(2,1)}), bf16[512,1024]{1,0:T(8,128)(2,1)}) %all-gather.12.cloned.1.call-update) | async-done | bytes 1048592 | tf_op jit(solution)/shard_map/all_gather | solution.py:129
  192.9 11.4 %all-gather.10.cloned.1.call-done = bf16[2048,512]{1,0:T(8,128)(2,1)} async-done(((bf16[1024,512]{1,0:T(8,128)(2,1)}), bf16[2048,512]{1,0:T(8,128)(2,1)}) %all-gather.10.cloned.1.call-update) | async-done | bytes 2097168 | tf_op jit(solution)/shard_map/all_gather | solution.py:33
  204.3 10.5 %multiply_convert_fusion.2 = (bf16[2048,1024]{1,0:T(8,128)(2,1)}, f32[2048,1024]{1,0:T(8,128)}) fusion(f32[1024]{0:T(1024)S(1)} %copy-done.22, bf16[2048,512]{1,0:T(8,128)(2,1)} %all-gather.10.cloned.1.call-done, bf16[512,1024]{1,0:T(8,128)(2,1)} %all-gather.12.cloned.1.call-done), kind=kOutput, calls=%fused_computation.129 | convolution fusion | flops 2168455168 | bytes 15732736 | tf_op jit(solution)/shard_map/dot_general | solution.py:177
  214.8 49.1 %all-gather.14.cloned.1.call-done = bf16[1024,512]{0,1:T(8,128)(2,1)} async-done(((bf16[1024,32]{0,1:T(8,128)(2,1)}), bf16[1024,512]{0,1:T(8,128)(2,1)}) %all-gather.14.cloned.1.call-update) | async-done | bytes 1048592 | tf_op jit(solution)/shard_map/all_gather | solution.py:130
  263.9 11.0 %all-gather.18.cloned.1.call-done = bf16[1,2048,512]{2,1,0:T(8,128)(2,1)} async-done(((bf16[1,1024,512]{2,1,0:T(8,128)(2,1)}), bf16[1,2048,512]{2,1,0:T(8,128)(2,1)}) %all-gather.18.cloned.1.call-update) | async-done | bytes 2097168 | tf_op jit(solution)/shard_map/all_gather | solution.py:33
  274.9 10.2 %convert_reduce_fusion = (f32[1024]{0:T(1024)S(1)}, bf16[2048,1024]{1,0:T(8,128)(2,1)S(1)}) fusion(f32[2048,1024]{1,0:T(8,128)} %get-tuple-element.582, f32[1024]{0:T(1024)S(1)} %copy-done.22, bf16[1024,512]{0,1:T(8,128)(2,1)} %all-gather.14.cloned.1.call-done, bf16[1,2048,512]{2,1,0:T(8,128)(2,1)} %all-gather.18.cloned.1.call-done), kind=kOutput, calls=%fused_computation.128 | convolution fusion | flops 2195717120 | bytes 15736832 | tf_op jit(solution)/shard_map/sd,fd->sf/dot_general | solution.py:190
  287.0 3.8 convolution_convert_fusion.1
  291.1 6.2 convolution_convert_fusion.2
  297.4 4.4 reduce-scatter.13.cloned.1.call-done
  304.7 10.0 %reduce-scatter.11.cloned.1.call-done = bf16[1024,512]{1,0:T(8,128)(2,1)} async-done(((bf16[2048,512]{1,0:T(8,128)(2,1)}), bf16[1024,512]{1,0:T(8,128)(2,1)}) %reduce-scatter.11.cloned.1.call-update) | async-done | bytes 1048592 | tf_op jit(solution)/shard_map/reduce_scatter | solution.py:37
  314.7 4.2 convert_reduce_fusion.3
  319.0 6.6 fusion.131
  325.7 7.2 %fusion.155 = f32[512,1024]{1,0:T(8,128)} fusion(bf16[2048,512]{1,0:T(8,128)(2,1)} %all-gather.10.cloned.1.call-done, bf16[2048,1024]{1,0:T(8,128)(2,1)} %copy-done.25), kind=kOutput, calls=%fused_computation.228 | convolution fusion | flops 2147483648 | bytes 8388608 | tf_op jit(solution)/shard_map/sd,sf->df/dot_general | solution.py:193
  333.2 3.3 convolution_convert_fusion.5
  341.4 32.6 %while.51 = (s32[]{:T(128)}, bf16[4,8,256,64]{2,3,0,1:T(8,128)(2,1)}, f32[4,8,256,64]{2,3,0,1:T(8,128)}, f32[4,8,256,64]{2,3,0,1:T(8,128)}, f32[4,16,64]{2,1,0:T...) while((s32[]{:T(128)}, ...), condition=%wide.region_21.22_spmd.clone, body=%wide.region_18.21_spmd.clone.sunk | while | flops 361561216 | bytes 22604664 | solution.py:224
  374.0 3.6 fusion.154
  387.5 3.0 fusion.127
  390.9 5.0 convolution_convert_fusion.4
  397.7 17.2 %reduce-scatter.23.cloned.1.call-done = f32[1024,32]{0,1:T(8,128)} async-done(((f32[1024,512]{0,1:T(8,128)}), f32[1024,32]{0,1:T(8,128)}) %reduce-scatter.23.cloned.1.call-update) | async-done | bytes 131088 | tf_op jit(solution)/shard_map/reduce_scatter | solution.py:267
  416.5 78.2 %reduce-scatter.21.cloned.1.call-done = f32[32,1024]{1,0:T(8,128)} async-done(((f32[512,1024]{1,0:T(8,128)}), f32[32,1024]{1,0:T(8,128)}) %reduce-scatter.21.cloned.1.call-update) | async-done | bytes 131088 | tf_op jit(solution)/shard_map/reduce_scatter | solution.py:266
  496.2 74.7 %reduce-scatter.19.cloned.1.call-done = f32[256,32]{0,1:T(8,128)} async-done(((f32[256,512]{0,1:T(8,128)}), f32[256,32]{0,1:T(8,128)}) %reduce-scatter.19.cloned.1.call-update) | async-done | bytes 32784 | tf_op jit(solution)/shard_map/reduce_scatter | solution.py:265
  572.3 76.1 %reduce-scatter.17.cloned.1.call-done = f32[32,3,256]{2,0,1:T(8,128)} async-done(((f32[512,3,256]{2,0,1:T(8,128)}), f32[32,3,256]{2,0,1:T(8,128)}) %reduce-scatter.17.cloned.1.call-update) | async-done | bytes 98320 | tf_op jit(solution)/shard_map/reduce_scatter | solution.py:264
  650.0 7.2 %reduce-scatter.15.cloned.1.call-done = bf16[1024,512]{1,0:T(8,128)(2,1)} async-done(((bf16[2048,512]{1,0:T(8,128)(2,1)}), bf16[1024,512]{1,0:T(8,128)(2,1)}) %reduce-scatter.15.cloned.1.call-update) | async-done | bytes 1048592 | tf_op jit(solution)/shard_map/reduce_scatter | solution.py:37
  659.8 40.7 %all-reduce = (f32[512]{0:T(512)S(1)}, f32[512]{0:T(512)S(1)}, f32[512]{0:T(512)S(1)}, f32[2048]{0:T(1024)S(1)}, f32[512]{0:T(512)S(1)}) all-reduce(f32[512]{0:T(512)S(1)} %get-tuple-element.489, f32[512]{0:T(512)S(1)} %get-tuple-element.564, f32[512]{0:T(512)S(1)} %get-tuple-element.487, ...), channel_id=1, replica_groups=mesh['dp'=16,'tensor'=2] {'dp','tensor'}, use_global_device_ids=true, to_apply=%region_26.27 | all-reduce | flops 4096 | bytes 32768 | tf_op jit(solution)/shard_map/psum | solution.py:253
  703.5 2.9 fusion.140
  (250 shorter events, 104.8 us)
Async XLA Ops:
  8.0 3.3 copy-start
  8.0 3.3 copy-start.16
  8.0 89.3 %all-gather.8.cloned.1.call-start = ((), (), s32[]{:S(2)}) async-start(), calls=%async_computation.8 | async-start | bytes 3145728 | tf_op jit(solution)/shard_map/all_gather | solution.py:33
  9.6 3.3 copy-start.12
  9.6 3.4 copy-start.14
  12.8 47.6 %copy-start.18 = (bf16[256,32]{0,1:T(8,128)(2,1)S(1)}, bf16[256,32]{0,1:T(8,128)(2,1)}, u32[]{:S(2)}) copy-start(bf16[256,32]{0,1:T(8,128)(2,1)} %param.23) | copy-start | bytes 49156
  12.8 130.9 %reduce-scatter.9.cloned.1.call-start = ((), (), s32[]{:S(2)}) async-start(), calls=%async_computation.9 | async-start | bytes 3145728 | tf_op jit(solution)/shard_map/reduce_scatter | solution.py:37
  60.4 42.1 %copy-start.10 = (bf16[512,3,256]{0,2,1:T(8,128)(2,1)}, bf16[512,3,256]{0,2,1:T(8,128)(2,1)S(1)}, u32[]{:S(2)}) copy-start(bf16[512,3,256]{0,2,1:T(8,128)(2,1)S(1)} %copy.63) | copy-start | bytes 2359300
  130.4 2.5 copy-start.23
  133.9 9.7 %copy-start.13 = (f32[512]{0:T(512)S(1)}, f32[512]{0:T(512)}, u32[]{:S(2)}) copy-start(f32[512]{0:T(512)} %param.24) | copy-start | bytes 6148
  136.1 56.8 %all-gather.12.cloned.1.call-start = ((), (), s32[]{:S(2)}) async-start(), calls=%async_computation.11 | async-start | bytes 1114112 | tf_op jit(solution)/shard_map/all_gather | solution.py:129
  136.7 9.4 %copy-start.17 = (f32[512]{0:T(512)S(1)}, f32[512]{0:T(512)}, u32[]{:S(2)}) copy-start(f32[512]{0:T(512)} %param.25) | copy-start | bytes 6148
  136.7 67.6 %all-gather.10.cloned.1.call-start = ((), (), s32[]{:S(2)}) async-start(), calls=%async_computation.10 | async-start | bytes 3145728 | tf_op jit(solution)/shard_map/all_gather | solution.py:33
  146.1 58.2 %copy-start.22 = (f32[1024]{0:T(1024)S(1)}, f32[1024]{0:T(1024)}, u32[]{:S(2)}) copy-start(f32[1024]{0:T(1024)} %param.27) | copy-start | bytes 12292
  147.6 116.3 %all-gather.14.cloned.1.call-start = ((), (), s32[]{:S(2)}) async-start(), calls=%async_computation.12 | async-start | bytes 1114112 | tf_op jit(solution)/shard_map/all_gather | solution.py:130
  148.2 126.7 %all-gather.18.cloned.1.call-start = ((), (), s32[]{:S(2)}) async-start(), calls=%async_computation.21 | async-start | bytes 3145728 | tf_op jit(solution)/shard_map/all_gather | solution.py:33
  148.9 152.9 %reduce-scatter.13.cloned.1.call-start = ((), (), s32[]{:S(2)}) async-start(), calls=%async_computation.14 | async-start | bytes 3145728 | tf_op jit(solution)/shard_map/reduce_scatter | solution.py:37
  274.9 12.1 %copy-start.21 = (bf16[512,1024]{1,0:T(8,128)(2,1)S(1)}, bf16[512,1024]{1,0:T(8,128)(2,1)}, u32[]{:S(2)}) copy-start(bf16[512,1024]{1,0:T(8,128)(2,1)} %all-gather.12.cloned.1.call-done) | copy-start | bytes 3145732
  290.9 23.9 %reduce-scatter.11.cloned.1.call-start = ((), (), s32[]{:S(2)}) async-start(), calls=%async_computation.13 | async-start | bytes 3145728 | tf_op jit(solution)/shard_map/reduce_scatter | solution.py:37
  297.3 17.4 %copy-start.19 = (f32[512]{0:T(512)S(1)}, f32[512]{0:T(512)}, u32[]{:S(2)}) copy-start(f32[512]{0:T(512)} %param.29) | copy-start | bytes 6148
  297.4 35.9 %all-gather.16.cloned.1.call-start = ((), (), s32[]{:S(2)}) async-start(), calls=%async_computation.15 | async-start | bytes 3145728 | tf_op jit(solution)/shard_map/all_gather | solution.py:33
  318.9 95.9 %reduce-scatter.23.cloned.1.call-start = ((), (), s32[]{:S(2)}) async-start(), calls=%async_computation.20 | async-start | bytes 2228224 | tf_op jit(solution)/shard_map/reduce_scatter | solution.py:267
  325.6 169.1 %reduce-scatter.21.cloned.1.call-start = ((), (), s32[]{:S(2)}) async-start(), calls=%async_computation.19 | async-start | bytes 2228224 | tf_op jit(solution)/shard_map/reduce_scatter | solution.py:266
  332.9 238.1 %reduce-scatter.19.cloned.1.call-start = ((), (), s32[]{:S(2)}) async-start(), calls=%async_computation.18 | async-start | bytes 557056 | tf_op jit(solution)/shard_map/reduce_scatter | solution.py:265
  336.5 4.9 copy-start.3
  336.5 4.9 copy-start.15
  336.5 4.9 copy-start.24
  377.7 270.8 %reduce-scatter.17.cloned.1.call-start = ((), (), s32[]{:S(2)}) async-start(), calls=%async_computation.17 | async-start | bytes 1671168 | tf_op jit(solution)/shard_map/reduce_scatter | solution.py:264
  384.7 2.8 copy-start.20
  387.5 3.4 copy-start.11
  390.6 266.6 %reduce-scatter.15.cloned.1.call-start = ((), (), s32[]{:S(2)}) async-start(), calls=%async_computation.16 | async-start | bytes 3145728 | tf_op jit(solution)/shard_map/reduce_scatter | solution.py:37
  657.2 46.3 %copy-start.6 = (bf16[1024,512]{1,0:T(8,128)(2,1)S(1)}, bf16[1024,512]{1,0:T(8,128)(2,1)}, u32[]{:S(2)}) copy-start(bf16[1024,512]{1,0:T(8,128)(2,1)} %reduce-scatter.15.cloned.1.call-done) | copy-start | bytes 3145732
  (8 other events, 13.4 us)
Sparse Core Ops, SparseCore 0:
  12.9 13.2 all-gather.7
  136.2 7.4 reduce-scatter.8
  291.0 10.8 reduce-scatter.12
  303.9 10.7 reduce-scatter.10
Sparse Core Ops, SparseCore 1:
  139.7 53.1 all-gather.11
  195.0 9.3 all-gather.9
  207.3 56.5 all-gather.13
  265.6 9.3 all-gather.17
  319.0 11.6 all-gather.15
  333.1 81.7 reduce-scatter.22
  417.1 77.5 reduce-scatter.20
  497.4 73.5 reduce-scatter.18
  573.1 75.3 reduce-scatter.16
  650.8 6.3 reduce-scatter.14
where the time goes:
time: 723 us; the launch traced here: 714 us
  waiting for transfers between devices  392 us (54%)
  blocking collectives  125 us (17%)
  matrix products  112 us (15%)
  other arithmetic  34.3 us (5%)
  local copies, waits for them, and re-layouts  32.8 us (5%)
  between operations  16.3 us (2%)
    reduce_scatter x1, waiting for transfers between devices, shards(): lax.psum_scatter(grad_up, 'dp', scatter_dimension=0, tiled=True)  78.2 us
    reduce_scatter x1, waiting for transfers between devices, shards(): lax.psum_scatter(grad_qkv, 'dp', scatter_dimension=0, tiled=True)  76.1 us
    reduce_scatter x1, waiting for transfers between devices, shards(): lax.psum_scatter(grad_wout, 'dp', scatter_dimension=1, tiled=True)  74.7 us
    all_gather x1, waiting for transfers between devices, shards(): lax.all_gather(w_down, 'dp', axis=1, tiled=True)  49.1 us
    all_gather x1, blocking collectives, shards(): lax.all_gather(w_qkv, 'dp', axis=0, tiled=True)  47 us
    all_gather x1, waiting for transfers between devices, shards(): lax.all_gather(w_up, 'dp', axis=0, tiled=True)  43.8 us
    psum x1, blocking collectives, shards(): lax.psum((gain_one_part, gain_two_part, jnp.sum(grad_branch, axis=0, dtyp...  40.7 us
    all_gather x1, blocking collectives, shards(): lax.all_gather(w_out, 'dp', axis=1, tiled=True)  36.9 us
  transfers between devices with their start and end apart: 14, of which 12 were waited for; matrix products, arithmetic and copies ran while one was open for 15% of the time, Pallas kernels for 0%

commit v1 on v0

--- a/solution.py
+++ b/solution.py
@@ -9,6 +9,27 @@
 SPB = 2
 epsilon = 1e-05
 masked = -1e30
+
+
+def collect(x, axis, dim):
+    size, index, width = (lax.axis_size(axis), lax.axis_index(axis), x.shape[dim])
+    right = [(i, (i + 1) % size) for i in range(size)]
+    downward = [(i, (i - 1) % size) for i in range(size)]
+    result = jnp.zeros((*x.shape[:dim], size * width, *x.shape[dim + 1 :]), x.dtype)
+    result = lax.dynamic_update_slice_in_dim(result, x, index * width, axis=dim)
+    from_left = from_right = x
+    half = size // 2
+    for turn in range(1, half + 1):
+        from_left = lax.ppermute(from_left, axis, right)
+        result = lax.dynamic_update_slice_in_dim(
+            result, from_left, (index - turn) % size * width, axis=dim
+        )
+        if turn < size - half:
+            from_right = lax.ppermute(from_right, axis, downward)
+            result = lax.dynamic_update_slice_in_dim(
+                result, from_right, (index + turn) % size * width, axis=dim
+            )
+    return result
 
 
 def normalize(values, gain_vec):
@@ -126,7 +147,7 @@
     full_qkv, full_out, full_up, full_down = (
         lax.all_gather(w_qkv, "dp", axis=0, tiled=True),
         lax.all_gather(w_out, "dp", axis=1, tiled=True),
-        lax.all_gather(w_up, "dp", axis=0, tiled=True),
+        collect(w_up, "dp", 0),
         lax.all_gather(w_down, "dp", axis=1, tiled=True),
     )
     unit_one, inverse_one, normed = normalize(incoming, gain_one)

time: 723 us -> 684 us (0.946)
  waiting for transfers between devices: 392 us -> 292 us
  starting transfers between devices: 1.53 us -> 42.7 us
  local copies, waits for them, and re-layouts: 32.8 us -> 48.5 us
    all_gather x1, waiting for transfers between devices: 49.1 us -> 0.01 us  [shards(): lax.all_gather(w_down, 'dp', axis=1, tiled=True)]
    all_gather x1 -> x0, waiting for transfers between devices: 43.8 us -> none  [shards(): lax.all_gather(w_up, 'dp', axis=0, tiled=True)]
    ppermute x0 -> x15, starting transfers between devices: none -> 41.3 us  [the longest x7 41.3 us: collect(): from_right = lax.ppermute(from_right, axis, downward)]
    all_gather x4, waiting for transfers between devices: 22.4 us -> 0.25 us  [pair_rows(): return lax.all_gather(values, 'tensor', axis=0, tiled=True)]
    ppermute x0 -> x15, waiting for transfers between devices: none -> 18 us  [the longest x8 15.8 us: collect(): from_left = lax.ppermute(from_left, axis, right)]
    dynamic_update_slice x0 -> x16, local copies, waits for them, and re-layouts: none -> 11.9 us  [the longest x8 5.94 us: collect(): lax.dynamic_update_slice_in_dim(result, from_left, (index - turn) % size...]
    unnamed x59 -> x61, local copies, waits for them, and re-layouts: 15.7 us -> 15.6 us
  transfers between devices with their start and end apart: 14 -> 28, of which waited for: 12 -> 18; matrix products, arithmetic and copies ran while one was open for 15% -> 17% of each run, Pallas kernels for 0% -> 0%
where the time goes in v1:
time: 684 us; the launch traced here: 674 us
  waiting for transfers between devices  292 us (43%)
  blocking collectives  125 us (18%)
  matrix products  114 us (17%)
  local copies, waits for them, and re-layouts  48.5 us (7%)
  starting transfers between devices  42.7 us (6%)
  other arithmetic  37 us (5%)
  between operations  14.9 us (2%)
    reduce_scatter x1, waiting for transfers between devices, shards(): lax.psum_scatter(grad_up, 'dp', scatter_dimension=0, tiled=True)  78 us
    reduce_scatter x1, waiting for transfers between devices, shards(): lax.psum_scatter(grad_qkv, 'dp', scatter_dimension=0, tiled=True)  76.4 us
    reduce_scatter x1, waiting for transfers between devices, shards(): lax.psum_scatter(grad_wout, 'dp', scatter_dimension=1, tiled=True)  75.2 us
    all_gather x1, blocking collectives, shards(): lax.all_gather(w_qkv, 'dp', axis=0, tiled=True)  47 us
    ppermute x7, starting transfers between devices, collect(): from_right = lax.ppermute(from_right, axis, downward)  41.3 us
    psum x1, blocking collectives, shards(): lax.psum((gain_one_part, gain_two_part, jnp.sum(grad_branch, axis=0, dtyp...  40.8 us
    all_gather x1, blocking collectives, shards(): lax.all_gather(w_out, 'dp', axis=1, tiled=True)  36.9 us
    reduce_scatter x4, waiting for transfers between devices, pair_sums(): lax.psum_scatter(term_fn(jnp.int32(0), rows * lax.axis_size('tensor')).as...  28.9 us
  transfers between devices with their start and end apart: 28, of which 18 were waited for; matrix products, arithmetic and copies ran while one was open for 17% of the time, Pallas kernels for 0%

profile of v1, /device:TPU:0, one launch (start us, length us, event | category | flops | bytes accessed | tf_op | source)
XLA Modules:
  0.0 674.2 jit_solution(10208905552175010667)
XLA Ops:
  12.2 47.0 %all_gather.22 = bf16[512,3,256]{2,0,1:T(8,128)(2,1)S(1)} all-gather(bf16[32,3,256]{2,0,1:T(8,128)(2,1)S(1)} %copy-done.15), channel_id=1, replica_groups=mesh['dp'=16,'tensor'=2] {'dp'}, dimensions={0}, use_global_device_ids=true | all-gather | bytes 835584 | tf_op jit(solution)/shard_map/all_gather | solution.py:148
  59.6 36.9 %all_gather.23 = bf16[256,512]{0,1:T(8,128)(2,1)S(1)} all-gather(bf16[256,32]{0,1:T(8,128)(2,1)S(1)} %copy-done.18), channel_id=1, replica_groups=mesh['dp'=16,'tensor'=2] {'dp'}, dimensions={1}, use_global_device_ids=true | all-gather | bytes 278528 | tf_op jit(solution)/shard_map/all_gather | solution.py:149
  96.5 5.0 convolution_convert_fusion
  101.6 4.7 copy.64
  115.0 17.0 %while.50 = (s32[]{:T(128)}, bf16[4,8,256,64]{2,3,1,0:T(8,128)(2,1)}, f32[4,8,256]{2,1,0:T(8,128)}, bf16[4,8,256,64]{2,3,1,0:T(8,128)(2,1)S(1)}, bf16[4,8,256,64...) while((s32[]{:T(128)}, ...), condition=%wide.region_10.11_spmd.clone, body=%wide.region_5.10_spmd.clone.sunk | while | flops 147880064 | bytes 9204541 | solution.py:186
  137.7 7.5 %reduce-scatter.9.cloned.1.call-done = bf16[1024,512]{1,0:T(8,128)(2,1)} async-done(((bf16[2048,512]{1,0:T(8,128)(2,1)}), bf16[1024,512]{1,0:T(8,128)(2,1)}) %reduce-scatter.9.cloned.1.call-update) | async-done | bytes 1048592 | tf_op jit(solution)/shard_map/reduce_scatter | solution.py:58
  149.7 5.5 collective-permute-start.1
  157.4 5.8 collective-permute-start.3
  166.2 5.8 collective-permute-start.5
  173.9 6.1 collective-permute-start.7
  181.9 6.1 collective-permute-start.9
  189.9 6.0 collective-permute-start.11
  197.8 6.1 collective-permute-start.13
  206.0 6.8 %collective-permute-done.12 = bf16[32,1024]{1,0:T(8,128)(2,1)S(1)} collective-permute-done((bf16[32,1024]{1,0:T(8,128)(2,1)S(1)}, bf16[32,1024]{1,0:T(8,128)(2,1)S(1)}, u32[]{:S(2)}, u32[]{:S(2)}) %collective-permute-start.12) | collective-permute-done | bytes 65568 | tf_op jit(solution)/shard_map/ppermute | solution.py:23
  214.1 7.7 %collective-permute-done.14 = bf16[32,1024]{1,0:T(8,128)(2,1)S(1)} collective-permute-done((bf16[32,1024]{1,0:T(8,128)(2,1)S(1)}, bf16[32,1024]{1,0:T(8,128)(2,1)S(1)}, u32[]{:S(2)}, u32[]{:S(2)}) %collective-permute-start.14) | collective-permute-done | bytes 65568 | tf_op jit(solution)/shard_map/ppermute | solution.py:23
  222.4 10.9 %multiply_convert_fusion.2 = (bf16[2048,1024]{1,0:T(8,128)(2,1)}, f32[2048,1024]{1,0:T(8,128)}) fusion(f32[1024]{0:T(1024)S(1)} %copy-done.23, bf16[2048,512]{1,0:T(8,128)(2,1)} %all-gather.9.cloned.1.call-done, bf16[512,1024]{1,0:T(8,128)(2,1)} %constant_dynamic-update-slice_fusion.2), kind=kOutput, calls=%fused_computation.129 | convolution fusion | flops 2168455168 | bytes 15732736 | tf_op jit(solution)/shard_map/dot_general | solution.py:198
  233.5 10.7 %convert_reduce_fusion = (f32[1024]{0:T(1024)}, bf16[2048,1024]{1,0:T(8,128)(2,1)S(1)}) fusion(f32[2048,1024]{1,0:T(8,128)} %get-tuple-element.582, f32[1024]{0:T(1024)S(1)} %copy-done.23, bf16[1024,512]{0,1:T(8,128)(2,1)} %all-gather.11.cloned.1.call-done, bf16[1,2048,512]{2,1,0:T(8,128)(2,1)} %all-gather.15.cloned.1.call-done), kind=kOutput, calls=%fused_computation.128 | convolution fusion | flops 2195717120 | bytes 15736832 | tf_op jit(solution)/shard_map/sd,fd->sf/dot_general | solution.py:211
  246.2 5.0 convolution_convert_fusion.1
  251.5 6.2 convolution_convert_fusion.2
  257.8 4.4 reduce-scatter.13.cloned.1.call-done
  265.1 10.1 %reduce-scatter.11.cloned.1.call-done = bf16[1024,512]{1,0:T(8,128)(2,1)} async-done(((bf16[2048,512]{1,0:T(8,128)(2,1)}), bf16[1024,512]{1,0:T(8,128)(2,1)}) %reduce-scatter.11.cloned.1.call-update) | async-done | bytes 1048592 | tf_op jit(solution)/shard_map/reduce_scatter | solution.py:58
  275.2 4.8 convert_reduce_fusion.3
  280.0 6.6 fusion.131
  286.7 7.1 %fusion.155 = f32[512,1024]{1,0:T(8,128)} fusion(bf16[2048,512]{1,0:T(8,128)(2,1)} %all-gather.9.cloned.1.call-done, bf16[2048,1024]{1,0:T(8,128)(2,1)} %copy-done.26), kind=kOutput, calls=%fused_computation.244 | convolution fusion | flops 2147483648 | bytes 8388608 | tf_op jit(solution)/shard_map/sd,sf->df/dot_general | solution.py:214
  302.5 35.4 %while.51 = (s32[]{:T(128)}, bf16[4,8,256,64]{2,3,0,1:T(8,128)(2,1)}, f32[4,8,256,64]{2,3,0,1:T(8,128)}, f32[4,8,256,64]{2,3,0,1:T(8,128)}, f32[4,16,64]{2,1,0:T...) while((s32[]{:T(128)}, ...), condition=%wide.region_21.22_spmd.clone, body=%wide.region_18.21_spmd.clone.sunk | while | flops 361561216 | bytes 22604664 | solution.py:245
  354.6 5.1 convolution_convert_fusion.4
  361.5 14.5 %reduce-scatter.23.cloned.1.call-done = f32[1024,32]{0,1:T(8,128)} async-done(((f32[1024,512]{0,1:T(8,128)}), f32[1024,32]{0,1:T(8,128)}) %reduce-scatter.23.cloned.1.call-update) | async-done | bytes 131088 | tf_op jit(solution)/shard_map/reduce_scatter | solution.py:288
  377.5 78.0 %reduce-scatter.21.cloned.1.call-done = f32[32,1024]{1,0:T(8,128)} async-done(((f32[512,1024]{1,0:T(8,128)}), f32[32,1024]{1,0:T(8,128)}) %reduce-scatter.21.cloned.1.call-update) | async-done | bytes 131088 | tf_op jit(solution)/shard_map/reduce_scatter | solution.py:287
  457.1 75.2 %reduce-scatter.19.cloned.1.call-done = f32[256,32]{0,1:T(8,128)} async-done(((f32[256,512]{0,1:T(8,128)}), f32[256,32]{0,1:T(8,128)}) %reduce-scatter.19.cloned.1.call-update) | async-done | bytes 32784 | tf_op jit(solution)/shard_map/reduce_scatter | solution.py:286
  533.6 76.4 %reduce-scatter.17.cloned.1.call-done = f32[32,3,256]{2,0,1:T(8,128)} async-done(((f32[512,3,256]{2,0,1:T(8,128)}), f32[32,3,256]{2,0,1:T(8,128)}) %reduce-scatter.17.cloned.1.call-update) | async-done | bytes 98320 | tf_op jit(solution)/shard_map/reduce_scatter | solution.py:285
  611.6 6.9 %reduce-scatter.15.cloned.1.call-done = bf16[1024,512]{1,0:T(8,128)(2,1)} async-done(((bf16[2048,512]{1,0:T(8,128)(2,1)}), bf16[1024,512]{1,0:T(8,128)(2,1)}) %reduce-scatter.15.cloned.1.call-update) | async-done | bytes 1048592 | tf_op jit(solution)/shard_map/reduce_scatter | solution.py:58
  621.1 40.8 %all-reduce = (f32[512]{0:T(512)S(1)}, f32[512]{0:T(512)S(1)}, f32[512]{0:T(512)S(1)}, f32[2048]{0:T(1024)S(1)}, f32[512]{0:T(512)S(1)}) all-reduce(f32[512]{0:T(512)S(1)} %get-tuple-element.489, f32[512]{0:T(512)S(1)} %copy-done.19, f32[512]{0:T(512)S(1)} %get-tuple-element.487, ...), channel_id=1, replica_groups=mesh['dp'=16,'tensor'=2] {'dp','tensor'}, use_global_device_ids=true, to_apply=%region_26.27 | all-reduce | flops 4096 | bytes 32768 | tf_op jit(solution)/shard_map/psum | solution.py:274
  (296 shorter events, 140.9 us)
Async XLA Ops:
  7.2 89.3 %all-gather.7.cloned.1.call-start = ((), (), s32[]{:S(2)}) async-start(), calls=%async_computation.8 | async-start | bytes 3145728 | tf_op jit(solution)/shard_map/all_gather | solution.py:54
  11.9 47.6 %copy-start.18 = (bf16[256,32]{0,1:T(8,128)(2,1)S(1)}, bf16[256,32]{0,1:T(8,128)(2,1)}, u32[]{:S(2)}) copy-start(bf16[256,32]{0,1:T(8,128)(2,1)} %param.23) | copy-start | bytes 49156
  12.0 133.2 %reduce-scatter.9.cloned.1.call-start = ((), (), s32[]{:S(2)}) async-start(), calls=%async_computation.9 | async-start | bytes 3145728 | tf_op jit(solution)/shard_map/reduce_scatter | solution.py:58
  137.6 84.8 %all-gather.9.cloned.1.call-start = ((), (), s32[]{:S(2)}) async-start(), calls=%async_computation.10 | async-start | bytes 3145728 | tf_op jit(solution)/shard_map/all_gather | solution.py:54
  149.1 84.2 %all-gather.11.cloned.1.call-start = ((), (), s32[]{:S(2)}) async-start(), calls=%async_computation.11 | async-start | bytes 1114112 | tf_op jit(solution)/shard_map/all_gather | solution.py:151
  149.7 72.8 %copy-start.23 = (f32[1024]{0:T(1024)S(1)}, f32[1024]{0:T(1024)}, u32[]{:S(2)}) copy-start(f32[1024]{0:T(1024)} %param.27) | copy-start | bytes 12292
  149.7 83.9 %all-gather.15.cloned.1.call-start = ((), (), s32[]{:S(2)}) async-start(), calls=%async_computation.20 | async-start | bytes 3145728 | tf_op jit(solution)/shard_map/all_gather | solution.py:54
  149.7 7.6 %collective-permute-start.1 = (bf16[32,1024]{1,0:T(8,128)(2,1)S(1)}, bf16[32,1024]{1,0:T(8,128)(2,1)}, u32[]{:S(2)}, u32[]{:S(2)}) collective-permute-start(bf16[32,1024]{1,0:T(8,128)(2,1)S(1)} %copy-done.13), channel_id=1, source_target_pairs={{0,30},{2,0},{4,2},{6,4},{8,6},{10,8},{12,10},{14,12},{16,14},{18,... | collective-permute-start | bytes 196616 | tf_op jit(solution)/shard_map/ppermute | solution.py:28
  155.2 8.0 %collective-permute-start = (bf16[32,1024]{1,0:T(8,128)(2,1)S(1)}, bf16[32,1024]{1,0:T(8,128)(2,1)}, u32[]{:S(2)}, u32[]{:S(2)}) collective-permute-start(bf16[32,1024]{1,0:T(8,128)(2,1)S(1)} %copy-done.13), channel_id=1, source_target_pairs={{0,2},{2,4},{4,6},{6,8},{8,10},{10,12},{12,14},{14,16},{16,18},{18... | collective-permute-start | bytes 196616 | tf_op jit(solution)/shard_map/ppermute | solution.py:23
  155.3 106.9 %reduce-scatter.13.cloned.1.call-start = ((), (), s32[]{:S(2)}) async-start(), calls=%async_computation.13 | async-start | bytes 3145728 | tf_op jit(solution)/shard_map/reduce_scatter | solution.py:58
  157.4 8.8 %collective-permute-start.3 = (bf16[32,1024]{1,0:T(8,128)(2,1)}, bf16[32,1024]{1,0:T(8,128)(2,1)S(1)}, u32[]{:S(2)}, u32[]{:S(2)}) collective-permute-start(bf16[32,1024]{1,0:T(8,128)(2,1)} %collective-permute-done.1), channel_id=1, source_target_pairs={{0,30},{2,0},{4,2},{6,4},{8,6},{10,8},{12,10},{14,12},{16,14},{18,... | collective-permute-start | bytes 196616 | tf_op jit(solution)/shard_map/ppermute | solution.py:28
  163.2 8.8 %collective-permute-start.2 = (bf16[32,1024]{1,0:T(8,128)(2,1)}, bf16[32,1024]{1,0:T(8,128)(2,1)S(1)}, u32[]{:S(2)}, u32[]{:S(2)}) collective-permute-start(bf16[32,1024]{1,0:T(8,128)(2,1)} %collective-permute-done), channel_id=1, source_target_pairs={{0,2},{2,4},{4,6},{6,8},{8,10},{10,12},{12,14},{14,16},{16,18},{18... | collective-permute-start | bytes 196616 | tf_op jit(solution)/shard_map/ppermute | solution.py:23
  166.2 7.7 %collective-permute-start.5 = (bf16[32,1024]{1,0:T(8,128)(2,1)S(1)}, bf16[32,1024]{1,0:T(8,128)(2,1)S(1)}, u32[]{:S(2)}, u32[]{:S(2)}) collective-permute-start(bf16[32,1024]{1,0:T(8,128)(2,1)S(1)} %collective-permute-done.3), channel_id=1, source_target_pairs={{0,30},{2,0},{4,2},{6,4},{8,6},{10,8},{12,10},{14,12},{16,14},{18,... | collective-permute-start | bytes 196616 | tf_op jit(solution)/shard_map/ppermute | solution.py:28
  172.0 8.0 %collective-permute-start.4 = (bf16[32,1024]{1,0:T(8,128)(2,1)S(1)}, bf16[32,1024]{1,0:T(8,128)(2,1)S(1)}, u32[]{:S(2)}, u32[]{:S(2)}) collective-permute-start(bf16[32,1024]{1,0:T(8,128)(2,1)S(1)} %collective-permute-done.2), channel_id=1, source_target_pairs={{0,2},{2,4},{4,6},{6,8},{8,10},{10,12},{12,14},{14,16},{16,18},{18... | collective-permute-start | bytes 196616 | tf_op jit(solution)/shard_map/ppermute | solution.py:23
  173.9 8.0 %collective-permute-start.7 = (bf16[32,1024]{1,0:T(8,128)(2,1)S(1)}, bf16[32,1024]{1,0:T(8,128)(2,1)S(1)}, u32[]{:S(2)}, u32[]{:S(2)}) collective-permute-start(bf16[32,1024]{1,0:T(8,128)(2,1)S(1)} %collective-permute-done.5), channel_id=1, source_target_pairs={{0,30},{2,0},{4,2},{6,4},{8,6},{10,8},{12,10},{14,12},{16,14},{18,... | collective-permute-start | bytes 196616 | tf_op jit(solution)/shard_map/ppermute | solution.py:28
  180.0 8.1 %collective-permute-start.6 = (bf16[32,1024]{1,0:T(8,128)(2,1)S(1)}, bf16[32,1024]{1,0:T(8,128)(2,1)S(1)}, u32[]{:S(2)}, u32[]{:S(2)}) collective-permute-start(bf16[32,1024]{1,0:T(8,128)(2,1)S(1)} %collective-permute-done.4), channel_id=1, source_target_pairs={{0,2},{2,4},{4,6},{6,8},{8,10},{10,12},{12,14},{14,16},{16,18},{18... | collective-permute-start | bytes 196616 | tf_op jit(solution)/shard_map/ppermute | solution.py:23
  181.9 8.0 %collective-permute-start.9 = (bf16[32,1024]{1,0:T(8,128)(2,1)S(1)}, bf16[32,1024]{1,0:T(8,128)(2,1)S(1)}, u32[]{:S(2)}, u32[]{:S(2)}) collective-permute-start(bf16[32,1024]{1,0:T(8,128)(2,1)S(1)} %collective-permute-done.7), channel_id=1, source_target_pairs={{0,30},{2,0},{4,2},{6,4},{8,6},{10,8},{12,10},{14,12},{16,14},{18,... | collective-permute-start | bytes 196616 | tf_op jit(solution)/shard_map/ppermute | solution.py:28
  188.1 8.0 %collective-permute-start.8 = (bf16[32,1024]{1,0:T(8,128)(2,1)S(1)}, bf16[32,1024]{1,0:T(8,128)(2,1)S(1)}, u32[]{:S(2)}, u32[]{:S(2)}) collective-permute-start(bf16[32,1024]{1,0:T(8,128)(2,1)S(1)} %collective-permute-done.6), channel_id=1, source_target_pairs={{0,2},{2,4},{4,6},{6,8},{8,10},{10,12},{12,14},{14,16},{16,18},{18... | collective-permute-start | bytes 196616 | tf_op jit(solution)/shard_map/ppermute | solution.py:23
  189.9 7.9 %collective-permute-start.11 = (bf16[32,1024]{1,0:T(8,128)(2,1)S(1)}, bf16[32,1024]{1,0:T(8,128)(2,1)S(1)}, u32[]{:S(2)}, u32[]{:S(2)}) collective-permute-start(bf16[32,1024]{1,0:T(8,128)(2,1)S(1)} %collective-permute-done.9), channel_id=1, source_target_pairs={{0,30},{2,0},{4,2},{6,4},{8,6},{10,8},{12,10},{14,12},{16,14},{18,... | collective-permute-start | bytes 196616 | tf_op jit(solution)/shard_map/ppermute | solution.py:28
  196.1 8.7 %collective-permute-start.10 = (bf16[32,1024]{1,0:T(8,128)(2,1)S(1)}, bf16[32,1024]{1,0:T(8,128)(2,1)S(1)}, u32[]{:S(2)}, u32[]{:S(2)}) collective-permute-start(bf16[32,1024]{1,0:T(8,128)(2,1)S(1)} %collective-permute-done.8), channel_id=1, source_target_pairs={{0,2},{2,4},{4,6},{6,8},{8,10},{10,12},{12,14},{14,16},{16,18},{18... | collective-permute-start | bytes 196616 | tf_op jit(solution)/shard_map/ppermute | solution.py:23
  197.8 15.7 %collective-permute-start.13 = (bf16[32,1024]{1,0:T(8,128)(2,1)S(1)}, bf16[32,1024]{1,0:T(8,128)(2,1)S(1)}, u32[]{:S(2)}, u32[]{:S(2)}) collective-permute-start(bf16[32,1024]{1,0:T(8,128)(2,1)S(1)} %collective-permute-done.11), channel_id=1, source_target_pairs={{0,30},{2,0},{4,2},{6,4},{8,6},{10,8},{12,10},{14,12},{16,14},{18,... | collective-permute-start | bytes 196616 | tf_op jit(solution)/shard_map/ppermute | solution.py:28
  204.7 8.0 %collective-permute-start.12 = (bf16[32,1024]{1,0:T(8,128)(2,1)S(1)}, bf16[32,1024]{1,0:T(8,128)(2,1)S(1)}, u32[]{:S(2)}, u32[]{:S(2)}) collective-permute-start(bf16[32,1024]{1,0:T(8,128)(2,1)S(1)} %collective-permute-done.10), channel_id=1, source_target_pairs={{0,2},{2,4},{4,6},{6,8},{8,10},{10,12},{12,14},{14,16},{16,18},{18... | collective-permute-start | bytes 196616 | tf_op jit(solution)/shard_map/ppermute | solution.py:23
  212.8 9.0 %collective-permute-start.14 = (bf16[32,1024]{1,0:T(8,128)(2,1)S(1)}, bf16[32,1024]{1,0:T(8,128)(2,1)S(1)}, u32[]{:S(2)}, u32[]{:S(2)}) collective-permute-start(bf16[32,1024]{1,0:T(8,128)(2,1)S(1)} %collective-permute-done.12), channel_id=1, source_target_pairs={{0,2},{2,4},{4,6},{6,8},{8,10},{10,12},{12,14},{14,16},{16,18},{18... | collective-permute-start | bytes 196616 | tf_op jit(solution)/shard_map/ppermute | solution.py:23
  251.2 24.0 %reduce-scatter.11.cloned.1.call-start = ((), (), s32[]{:S(2)}) async-start(), calls=%async_computation.12 | async-start | bytes 3145728 | tf_op jit(solution)/shard_map/reduce_scatter | solution.py:58
  257.7 36.6 %all-gather.13.cloned.1.call-start = ((), (), s32[]{:S(2)}) async-start(), calls=%async_computation.14 | async-start | bytes 3145728 | tf_op jit(solution)/shard_map/all_gather | solution.py:54
  280.0 96.0 %reduce-scatter.23.cloned.1.call-start = ((), (), s32[]{:S(2)}) async-start(), calls=%async_computation.19 | async-start | bytes 2228224 | tf_op jit(solution)/shard_map/reduce_scatter | solution.py:288
  286.6 168.9 %reduce-scatter.21.cloned.1.call-start = ((), (), s32[]{:S(2)}) async-start(), calls=%async_computation.18 | async-start | bytes 2228224 | tf_op jit(solution)/shard_map/reduce_scatter | solution.py:287
  293.9 238.4 %reduce-scatter.19.cloned.1.call-start = ((), (), s32[]{:S(2)}) async-start(), calls=%async_computation.17 | async-start | bytes 557056 | tf_op jit(solution)/shard_map/reduce_scatter | solution.py:286
  341.6 268.5 %reduce-scatter.17.cloned.1.call-start = ((), (), s32[]{:S(2)}) async-start(), calls=%async_computation.16 | async-start | bytes 1671168 | tf_op jit(solution)/shard_map/reduce_scatter | solution.py:285
  354.4 264.1 %reduce-scatter.15.cloned.1.call-start = ((), (), s32[]{:S(2)}) async-start(), calls=%async_computation.15 | async-start | bytes 3145728 | tf_op jit(solution)/shard_map/reduce_scatter | solution.py:58
  359.7 261.3 %copy-start.19 = (f32[512]{0:T(512)S(1)}, f32[512]{0:T(512)}, u32[]{:S(2)}) copy-start(f32[512]{0:T(512)} %get-tuple-element.564) | copy-start | bytes 6148
  361.1 303.6 %copy-start.5 = (f32[1024,512]{1,0:T(8,128)S(1)}, f32[1024,512]{1,0:T(8,128)}, u32[]{:S(2)}) copy-start(f32[1024,512]{1,0:T(8,128)} %get-tuple-element.566) | copy-start | bytes 6291460
  (23 other events, 127.8 us)
Sparse Core Ops, SparseCore 0:
  12.1 13.2 all-gather.6
  137.7 7.4 reduce-scatter.8
  149.2 11.7 all-gather.8
  164.0 57.9 all-gather.10
  223.5 9.9 all-gather.14
  251.3 10.7 reduce-scatter.12
  264.4 10.7 reduce-scatter.10
  280.1 11.7 all-gather.12
  294.3 81.6 reduce-scatter.22
  378.2 77.2 reduce-scatter.20
  458.4 73.7 reduce-scatter.18
  534.4 75.6 reduce-scatter.16
  612.4 6.0 reduce-scatter.14
